TPU v7x, 32 devices: a whole 2x2x4 slice. The times are simulated.
32 devices in a mesh: groups: 2 (over y), rows: 4 (over x, core), cols: 4 (over z).
Axes of the slice: x: 2, y: 2, z: 4, core: 2. Of those that a mesh axis runs over, the one named last changes fastest.
Arguments:
- pair_rep: float32 [384, 192, 128], P(('groups', 'cols'), 'rows'), parts along dimension 0, may hold values from -6 to 6
- token_mask: int32 [384], P(('groups', 'rows')), parts along dimension 0, may hold values from 0 to 1, as said below
- norm_gain: float32 [128], replicated, may hold values from 0.1 to 1.9
- norm_shift: float32 [128], replicated, may hold values from -3 to 3
- w_query: bfloat16 [128, 128], replicated, may hold values from -0.5 to 0.5
- w_keyval: bfloat16 [128, 256], replicated, may hold values from -0.5 to 0.5
- w_gate: bfloat16 [128, 128], replicated, may hold values from -0.5 to 0.5
- gate_shift: float32 [128], replicated, may hold values from -3 to 3
- w_bias: float32 [128, 4], replicated, may hold values from -12 to 12
- w_out: bfloat16 [128, 128], replicated, may hold values from -0.5 to 0.5
- out_shift: float32 [128], replicated, may hold values from -3 to 3
Outputs:
- pair_update: float32 [384, 192, 128], P(('groups', 'cols'), 'rows'), parts along dimension 0
There are 2 independent parts, one for each index of `groups`. A program takes and returns all parts, laid end to end along the dimension named above; an argument that names none is the same for every part. Nothing has to cross between parts.
Inputs may be any that keep to these rules, and one draw needn't show every extreme that they name: `token_mask`: position 0 is always a valid residue and the last position never is.
All inputs are finite; a program needn't handle non-finite values.
Results may differ from a plain program's by a relative error of at most 0.012.
The roundings to bfloat16 on the way count: a program that leaves them out, or rounds other values in their place, can miss the bound.
Values may be sent and summed in bfloat16 or wider, within the bound.
No kernel may reach another device: no remote copies, remote signals or barrier semaphores. Data moves between devices by JAX's collectives and lax.ppermute only.
A program may use at most 128 MiB of HBM per device.

v0:
```python
import jax
import jax.numpy as jnp
from jax import lax
from jax.sharding import PartitionSpec as P

HEADS = 4
HEAD_DIM = 32


def layer_norm(values, norm_gain, norm_shift):
    mean_val = jnp.mean(values, axis=-1, keepdims=True)
    centred = values - mean_val
    variance = jnp.mean(centred * centred, axis=-1, keepdims=True)
    return (centred * lax.rsqrt(variance + 1e-05) * norm_gain + norm_shift).astype(jnp.bfloat16)


def largest_divisor(count, limit):
    return max(
        (candidate for candidate in range(1, min(count, limit) + 1) if count % candidate == 0)
    )


def whole_row_layer(
    normed, token_mask, w_query, w_keyval, w_gate, gate_shift, w_bias, w_out, out_shift
):
    width = normed.shape[2]
    local_bias = jnp.dot(
        normed.astype(jnp.float32), w_bias, precision=lax.Precision.HIGHEST
    ).transpose(2, 0, 1)
    wide = lax.all_to_all(normed, "rows", split_axis=0, concat_axis=1, tiled=True)
    few_rows, token_count, _ = wide.shape
    bias_part = lax.all_gather(local_bias, "cols", axis=1, tiled=True)
    full_bias, full_mask = (
        lax.all_gather(bias_part, "rows", axis=2, tiled=True),
        lax.all_gather(token_mask.astype(jnp.float32), "rows", axis=0, tiled=True),
    )
    queries = (
        jnp.dot(wide, w_query, preferred_element_type=jnp.float32) * HEAD_DIM ** (-0.5)
    ).astype(jnp.bfloat16)
    queries = queries.reshape(few_rows, token_count, HEADS, HEAD_DIM)
    keyvals = jnp.dot(wide, w_keyval, preferred_element_type=jnp.float32).astype(jnp.bfloat16)
    keys = keyvals[..., :width].reshape(few_rows, token_count, HEADS, HEAD_DIM)
    values = keyvals[..., width:].reshape(few_rows, token_count, HEADS, HEAD_DIM)
    gates = jax.nn.sigmoid(jnp.dot(wide, w_gate, preferred_element_type=jnp.float32) + gate_shift)
    usable = full_mask > 0.5
    block_len = largest_divisor(token_count, 128)

    def one_block(block_index, gated_all):
        start = block_index * block_len
        query_block = lax.dynamic_slice_in_dim(queries, start, block_len, 1)
        bias_block = lax.dynamic_slice_in_dim(full_bias, start, block_len, 1)
        gate_block = lax.dynamic_slice_in_dim(gates, start, block_len, 1)
        scores = jnp.einsum(
            "ijhd,ikhd->hijk", query_block, keys, preferred_element_type=jnp.float32
        )
        scores = scores + bias_block[:, None]
        scores = jnp.where(usable[None, None, None, :], scores, jnp.float32(-1000000000.0))
        highest = jnp.max(scores, axis=-1, keepdims=True)
        expo = jnp.exp(scores - highest)
        total = jnp.sum(expo, axis=-1)
        weights = expo.astype(jnp.bfloat16)
        mixed = jnp.einsum("hijk,ikhd->ijhd", weights, values, preferred_element_type=jnp.float32)
        attended = mixed / total.transpose(1, 2, 0)[..., None]
        gated = (gate_block * attended.reshape(few_rows, block_len, width)).astype(jnp.bfloat16)
        return lax.dynamic_update_slice_in_dim(gated_all, gated, start, 1)

    gated_all = lax.fori_loop(
        0,
        token_count // block_len,
        one_block,
        jnp.zeros((few_rows, token_count, width), jnp.bfloat16),
    )
    gated_home = lax.all_to_all(gated_all, "rows", split_axis=1, concat_axis=0, tiled=True)
    return jnp.dot(gated_home, w_out, preferred_element_type=jnp.float32) + out_shift


def on_device(
    pair_rep,
    token_mask,
    norm_gain,
    norm_shift,
    w_query,
    w_keyval,
    w_gate,
    gate_shift,
    w_bias,
    w_out,
    out_shift,
):
    normed = layer_norm(pair_rep, norm_gain, norm_shift)
    return whole_row_layer(
        normed, token_mask, w_query, w_keyval, w_gate, gate_shift, w_bias, w_out, out_shift
    )


def solution(mesh):
    return jax.shard_map(
        on_device,
        mesh=mesh,
        in_specs=(
            P(("groups", "cols"), "rows", None),
            P(("groups", "rows")),
            P(),
            P(),
            P(),
            P(),
            P(),
            P(),
            P(),
            P(),
            P(),
        ),
        out_specs=P(("groups", "cols"), "rows", None),
        check_vma=False,
    )
```

profile of v0, /device:TPU:0, one launch (start us, length us, event | category | flops | bytes accessed | tf_op | source)
XLA Modules:
  0.0 85.9 jit_solution(3610924705760710887)
XLA Ops:
  0.0 1.7 %reduce_sum.31 = f32[48,48]{1,0:T(8,128)S(1)} reduce(f32[48,48,128]{2,1,0:T(8,128)} %param.13, f32[]{:T(128)} %constant.58.clone.1), dimensions={2}, to_apply=%region_0.0 | reduce | flops 292608 | bytes 1188868 | tf_op jit(solution)/shard_map/reduce_sum | solution.py:11
  1.8 0.7 multiply_reduce_fusion
  2.5 0.0 copy-start.7
  2.5 1.5 %add_convert_fusion = bf16[48,48,128]{2,1,0:T(8,128)(2,1)} fusion(f32[48,48,128]{2,1,0:T(8,128)S(1)} %copy-done.1, f32[128]{0:T(128)S(1)} %copy-done.8, f32[128]{0:T(128)S(1)} %copy-done.9, f32[48,48]{1,0:T(8,128)S(1)} %add_rsqrt_fusion, f32[48,48]{1,0:T(8,128)S(1)} %broadcast_multiply_fusion), kind=kLoop, calls=%fused_computation.31 | loop fusion | flops 1474560 | bytes 1788928 | tf_op jit(solution)/shard_map/convert_element_type | solution.py:14
  4.0 4.2 %all-to-all-start = ((bf16[48,48,128]{2,1,0:T(8,128)(2,1)}), bf16[48,48,128]{2,1,0:T(8,128)(2,1)S(1)}, u32[]{:S(2)}, u32[]{:S(2)}) async-start(bf16[48,48,128]{2,1,0:T(8,128)(2,1)} %add_convert_fusion), calls=%async_computation | async-start | bytes 1179648 | tf_op jit(solution)/shard_map/all_to_all | solution.py:30
  8.3 2.8 %convolution_bitcast_fusion = f32[4,48,48]{2,0,1:T(4,128)S(1)} fusion(bf16[48,48,128]{2,1,0:T(8,128)(2,1)} %add_convert_fusion, f32[128,4]{0,1:T(4,128)S(1)} %copy-done.7), kind=kOutput, calls=%fused_computation.33 | convolution fusion | flops 14155776 | bytes 628736 | tf_op jit(solution)/shard_map/dot_general | solution.py:27
  11.1 15.8 %all_gather.10 = f32[4,192,48]{2,0,1:T(4,128)S(1)} all-gather(f32[4,48,48]{2,0,1:T(4,128)S(1)} %convolution_bitcast_fusion), channel_id=1, replica_groups=mesh['groups'=2,'rows'=4,'cols'=4] {'cols'}, dimensions={1}, use_global_device_ids=true | all-gather | bytes 184320 | tf_op jit(solution)/shard_map/all_gather | solution.py:32
  27.0 0.2 copy.36
  27.2 0.6 dynamic-slice
  28.3 0.1 convert_dynamic-update-slice_fusion
  28.4 5.6 %all-reduce = f32[192]{0:T(256)S(1)} all-reduce(f32[192]{0:T(256)S(1)} %convert_dynamic-update-slice_fusion), channel_id=1, replica_groups=mesh['groups'=2,'rows'=4,'cols'=4] {'rows'}, use_global_device_ids=true, to_apply=%add | all-reduce | flops 192 | bytes 1536
  34.1 9.0 %all_gather.11 = f32[4,192,192]{1,0,2:T(4,128)S(1)} all-gather(f32[4,192,48]{1,0,2:T(4,128)S(1)} %copy.36), channel_id=1, replica_groups=mesh['groups'=2,'rows'=4,'cols'=4] {'rows'}, dimensions={2}, use_global_device_ids=true | all-gather | bytes 737280 | tf_op jit(solution)/shard_map/all_gather | solution.py:34
  43.1 0.0 all-to-all-done
  43.1 0.1 copy.33
  43.2 0.4 convolution_convert_fusion
  43.7 0.3 fusion.39
  44.0 0.3 copy.35
  44.3 0.0 copy-start.6
  44.3 0.9 %copy.40 = bf16[12,192,4,32]{1,3,0,2:T(8,128)(2,1)} copy(bf16[12,192,4,32]{1,3,2,0:T(8,128)(2,1)S(1)} %bitcast.59) | data formatting | bytes 1179648 | tf_op jit(solution)/shard_map/while | solution.py:67
  45.2 1.2 %copy.37 = bf16[12,192,128]{1,2,0:T(8,128)(2,1)} copy(bf16[12,192,128]{2,1,0:T(8,128)(2,1)S(1)} %get-tuple-element.188) | data formatting | bytes 1179648 | tf_op jit(solution)/shard_map/slice | solution.py:43
  46.4 0.3 fusion.28
  46.7 1.2 %copy.34 = bf16[12,192,128]{1,2,0:T(8,128)(2,1)} copy(bf16[12,192,128]{2,1,0:T(8,128)(2,1)S(1)} %fusion.28) | data formatting | bytes 1179648 | tf_op jit(solution)/shard_map/convert_element_type | solution.py:39
  47.9 1.5 %fusion.27 = f32[12,192,128]{2,1,0:T(8,128)} fusion(bf16[12,192,128]{2,1,0:T(8,128)(2,1)S(1)} %bitcast.58, f32[128]{0:T(128)S(1)} %copy-done.13, bf16[128,128]{1,0:T(8,128)(2,1)S(1)} %copy-done.11), kind=kOutput, calls=%fused_computation.29 | convolution fusion | flops 76677120 | bytes 1802752 | tf_op jit(solution)/shard_map/dot_general | solution.py:44
  49.3 1.0 %broadcast_in_dim.45.clone = bf16[12,192,128]{2,0,1:T(8,128)(2,1)} broadcast(bf16[]{:T(256)} %constant.57.clone.1), dimensions={} | broadcast | bytes 589826 | tf_op jit(solution)/shard_map/broadcast_in_dim | solution.py:71
  50.3 18.9 %while.13 = (s32[]{:T(128)}, bf16[12,192,128]{2,0,1:T(8,128)(2,1)}, f32[12,192,128]{2,1,0:T(8,128)}, pred[192]{0:T(512)(128)(4,1)S(1)}, bf16[12,192,4,32]{1,3,2,...) while((s32[]{:T(128)}, bf16[12,192,128]{2,0,1:T(8,128)(2,1)}, ...), condition=%wide.region_5.6_spmd, body=%wide.region_2.5_spmd.sunk | while | flops 118112448 | bytes 19440052 | solution.py:67
  50.3 0.3 constant_dynamic-slice_fusion.13
  50.6 0.2 copy.78
  50.8 4.4 %fusion.59 = (f32[4,12,96]{2,1,0:T(8,128)S(1)}, bf16[4,12,96,192]{3,2,1,0:T(8,128)(2,1)}) fusion(f32[4,96,192]{2,1,0:T(8,128)S(1)} %copy.78, pred[192]{0:T(512)(128)(4,1)S(1)} %get-tuple-element.270, bf16[12,192,4,32]{1,3,0,2:T(8,128)(2,1)S(1)} %get-tuple-element.272, bf16[12,192,4,32]{1,3,2,0:T(8,128)(2,1)} %get-tuple-element.271, s32[]{:T(128)S(6)} %select_n.31), kind=kOutput, calls=%fused_computation.43.clone.1 | convolution fusion | flops 61046976 | bytes 3066052 | tf_op jit(solution)/shard_map/while/body/eval_jaxpr/sub | solution.py:59
  55.3 0.0 copy-start.2
  55.3 2.9 %fusion.60 = f32[12,96,4,32]{1,3,2,0:T(8,128)S(1)} fusion(bf16[12,192,4,32]{1,3,2,0:T(8,128)(2,1)} %get-tuple-element.274, bf16[4,12,96,192]{3,2,1,0:T(8,128)(2,1)} %get-tuple-element.241, f32[12,96,4]{1,2,0:T(4,128)S(1)} %copy.79), kind=kOutput, calls=%fused_computation.10.clone.1 | convolution fusion | flops 56770560 | bytes 2967552 | tf_op jit(solution)/shard_map/while/body/eval_jaxpr/hijk,ikhd->ijhd/dot_general | solution.py:62
  58.2 0.1 constant_dynamic-slice_fusion.12
  58.3 0.3 copy.77
  58.5 0.1 fusion.61
  58.6 0.3 copy.80
  59.0 0.8 constant_dynamic-update-slice_fusion.2
  59.8 0.3 constant_dynamic-slice_fusion.13
  60.1 0.2 copy.78
  60.3 4.4 %fusion.59 = (f32[4,12,96]{2,1,0:T(8,128)S(1)}, bf16[4,12,96,192]{3,2,1,0:T(8,128)(2,1)}) fusion(f32[4,96,192]{2,1,0:T(8,128)S(1)} %copy.78, pred[192]{0:T(512)(128)(4,1)S(1)} %get-tuple-element.270, bf16[12,192,4,32]{1,3,0,2:T(8,128)(2,1)S(1)} %get-tuple-element.272, bf16[12,192,4,32]{1,3,2,0:T(8,128)(2,1)} %get-tuple-element.271, s32[]{:T(128)S(6)} %select_n.31), kind=kOutput, calls=%fused_computation.43.clone.1 | convolution fusion | flops 61046976 | bytes 3066052 | tf_op jit(solution)/shard_map/while/body/eval_jaxpr/sub | solution.py:59
  64.7 0.0 copy-start.2
  64.7 2.9 %fusion.60 = f32[12,96,4,32]{1,3,2,0:T(8,128)S(1)} fusion(bf16[12,192,4,32]{1,3,2,0:T(8,128)(2,1)} %get-tuple-element.274, bf16[4,12,96,192]{3,2,1,0:T(8,128)(2,1)} %get-tuple-element.241, f32[12,96,4]{1,2,0:T(4,128)S(1)} %copy.79), kind=kOutput, calls=%fused_computation.10.clone.1 | convolution fusion | flops 56770560 | bytes 2967552 | tf_op jit(solution)/shard_map/while/body/eval_jaxpr/hijk,ikhd->ijhd/dot_general | solution.py:62
  67.6 0.1 constant_dynamic-slice_fusion.12
  67.7 0.3 copy.77
  68.0 0.1 fusion.61
  68.1 0.3 copy.80
  68.4 0.8 constant_dynamic-update-slice_fusion.2
  69.2 15.2 %all_to_all.36 = bf16[12,192,128]{2,0,1:T(8,128)(2,1)S(1)} all-to-all(bf16[12,192,128]{2,0,1:T(8,128)(2,1)} %get-tuple-element.281), channel_id=1, replica_groups=mesh['groups'=2,'rows'=4,'cols'=4] {'rows'}, dimensions={1} | all-to-all | bytes 1179648 | tf_op jit(solution)/shard_map/all_to_all | solution.py:73
  84.4 0.2 copy.44
  84.6 1.3 %convolution_add_fusion = f32[48,48,128]{2,1,0:T(8,128)} fusion(bf16[48,48,128]{2,1,0:T(8,128)(2,1)S(1)} %bitcast.62, f32[128]{0:T(128)S(1)} %copy-done.10, bf16[128,128]{1,0:T(8,128)(2,1)S(1)} %copy-done.5), kind=kOutput, calls=%fused_computation.23 | convolution fusion | flops 75792384 | bytes 1802752 | tf_op jit(solution)/shard_map/dot_general | solution.py:74
  (36 shorter events, 0.1 us)
Async XLA Ops:
  0.0 43.2 %copy-start = (bf16[128,256]{1,0:T(8,128)(2,1)S(1)}, bf16[128,256]{1,0:T(8,128)(2,1)}, u32[]{:S(2)}) copy-start(bf16[128,256]{1,0:T(8,128)(2,1)} %param.18) | copy-start | bytes 196612
  0.0 1.8 %copy-start.1 = (f32[48,48,128]{2,1,0:T(8,128)S(1)}, f32[48,48,128]{2,1,0:T(8,128)}, u32[]{:S(2)}) copy-start(f32[48,48,128]{2,1,0:T(8,128)} %param.13) | copy-start | bytes 3538948
  0.0 2.5 %copy-start.9 = (f32[128]{0:T(128)S(1)}, f32[128]{0:T(128)}, u32[]{:S(2)}) copy-start(f32[128]{0:T(128)} %param.15) | copy-start | bytes 1540
  0.0 2.5 %copy-start.8 = (f32[128]{0:T(128)S(1)}, f32[128]{0:T(128)}, u32[]{:S(2)}) copy-start(f32[128]{0:T(128)} %param.16) | copy-start | bytes 1540
  2.5 5.8 %copy-start.7 = (f32[128,4]{0,1:T(4,128)S(1)}, f32[128,4]{0,1:T(4,128)}, u32[]{:S(2)}) copy-start(f32[128,4]{0,1:T(4,128)} %param.21) | copy-start | bytes 6148
  4.0 39.1 %all-to-all-start = ((bf16[48,48,128]{2,1,0:T(8,128)(2,1)}), bf16[48,48,128]{2,1,0:T(8,128)(2,1)S(1)}, u32[]{:S(2)}, u32[]{:S(2)}) async-start(bf16[48,48,128]{2,1,0:T(8,128)(2,1)} %add_convert_fusion), calls=%async_computation | async-start | bytes 1179648 | tf_op jit(solution)/shard_map/all_to_all | solution.py:30
  8.3 18.9 %copy-start.14 = (u32[32]{0:T(128)S(1)}, u32[32]{0:T(128)}, u32[]{:S(2)}) copy-start(u32[32]{0:T(128)} %constant.66) | copy-start | bytes 388
  8.3 20.1 %copy-start.12 = (s32[48]{0:T(128)S(1)}, s32[48]{0:T(128)}, u32[]{:S(2)}) copy-start(s32[48]{0:T(128)} %param.14) | copy-start | bytes 580
  44.3 2.1 %copy-start.6 = (bf16[128,128]{1,0:T(8,128)(2,1)S(1)}, bf16[128,128]{1,0:T(8,128)(2,1)}, u32[]{:S(2)}) copy-start(bf16[128,128]{1,0:T(8,128)(2,1)} %param.17) | copy-start | bytes 98308
  46.4 1.5 %copy-start.11 = (bf16[128,128]{1,0:T(8,128)(2,1)S(1)}, bf16[128,128]{1,0:T(8,128)(2,1)}, u32[]{:S(2)}) copy-start(bf16[128,128]{1,0:T(8,128)(2,1)} %param.19) | copy-start | bytes 98308
  46.4 1.5 %copy-start.13 = (f32[128]{0:T(128)S(1)}, f32[128]{0:T(128)}, u32[]{:S(2)}) copy-start(f32[128]{0:T(128)} %param.20) | copy-start | bytes 1540
  47.9 2.5 %copy-start.3 = (bf16[12,192,4,32]{1,3,0,2:T(8,128)(2,1)S(1)}, bf16[12,192,4,32]{1,3,0,2:T(8,128)(2,1)}, u32[]{:S(2)}) copy-start(bf16[12,192,4,32]{1,3,0,2:T(8,128)(2,1)} %copy.40) | copy-start | bytes 1769476
  55.3 2.9 %copy-start.2 = (f32[12,192,128]{2,1,0:T(8,128)S(1)}, f32[12,192,128]{2,1,0:T(8,128)}, u32[]{:S(2)}) copy-start(f32[12,192,128]{2,1,0:T(8,128)} %get-tuple-element.269) | copy-start | bytes 3538948 | tf_op jit(solution)/shard_map/while
  58.6 1.2 %copy-start.4 = (bf16[12,192,4,32]{1,3,0,2:T(8,128)(2,1)S(1)}, bf16[12,192,4,32]{1,3,0,2:T(8,128)(2,1)}, u32[]{:S(2)}) copy-start(bf16[12,192,4,32]{1,3,0,2:T(8,128)(2,1)} %get-tuple-element.292) | copy-start | bytes 1769476 | tf_op jit(solution)/shard_map/while
  64.7 2.9 %copy-start.2 = (f32[12,192,128]{2,1,0:T(8,128)S(1)}, f32[12,192,128]{2,1,0:T(8,128)}, u32[]{:S(2)}) copy-start(f32[12,192,128]{2,1,0:T(8,128)} %get-tuple-element.269) | copy-start | bytes 3538948 | tf_op jit(solution)/shard_map/while
  68.1 1.1 %copy-start.4 = (bf16[12,192,4,32]{1,3,0,2:T(8,128)(2,1)S(1)}, bf16[12,192,4,32]{1,3,0,2:T(8,128)(2,1)}, u32[]{:S(2)}) copy-start(bf16[12,192,4,32]{1,3,0,2:T(8,128)(2,1)} %get-tuple-element.292) | copy-start | bytes 1769476 | tf_op jit(solution)/shard_map/while
  69.2 15.4 %copy-start.5 = (bf16[128,128]{1,0:T(8,128)(2,1)S(1)}, bf16[128,128]{1,0:T(8,128)(2,1)}, u32[]{:S(2)}) copy-start(bf16[128,128]{1,0:T(8,128)(2,1)} %param.22) | copy-start | bytes 98308
  69.2 15.4 %copy-start.10 = (f32[128]{0:T(128)S(1)}, f32[128]{0:T(128)}, u32[]{:S(2)}) copy-start(f32[128]{0:T(128)} %param.23) | copy-start | bytes 1540
where the time goes:
time: 86.4 us; the launch traced here: 85.9 us
  blocking collectives  45.7 us (53%)
  matrix products  21 us (24%)
  local copies, waits for them, and re-layouts  9.81 us (11%)
  other arithmetic  4.24 us (5%)
  starting transfers between devices  4.24 us (5%)
    all_gather x1, blocking collectives, whole_row_layer(): bias_part = lax.all_gather(local_bias, 'cols', axis=1, tiled=True)  15.8 us
    all_to_all x1, blocking collectives, whole_row_layer(): lax.all_to_all(gated_all, 'rows', split_axis=1, concat_axis=0, tiled=True)  15.2 us
    all_gather x1, blocking collectives, whole_row_layer(): lax.all_gather(bias_part, 'rows', axis=2, tiled=True)  9.04 us
    sub x2, matrix products, one_block(): expo = jnp.exp(scores - highest)  8.86 us
    dot_general x2, matrix products, one_block(): jnp.einsum('hijk,ikhd->ijhd', weights, values, preferred_element_type=jnp...  5.81 us
    unnamed x1, blocking collectives  5.63 us
    all_to_all x1, starting transfers between devices, whole_row_layer(): lax.all_to_all(normed, 'rows', split_axis=0, concat_axis=1, tiled=True)  4.24 us
    dot_general x1, matrix products, whole_row_layer(): jnp.dot(normed.astype(jnp.float32), w_bias, precision=lax.Precision.HIGHEST)  2.85 us
  transfers between devices with their start and end apart: 1, of which 0 were waited for; matrix products, arithmetic and copies ran while one was open for 4% of the time, Pallas kernels for 0%

commit v1 on v0

--- a/solution.py
+++ b/solution.py
@@ -29,7 +29,12 @@
     ).transpose(2, 0, 1)
     wide = lax.all_to_all(normed, "rows", split_axis=0, concat_axis=1, tiled=True)
     few_rows, token_count, _ = wide.shape
-    bias_part = lax.all_gather(local_bias, "cols", axis=1, tiled=True)
+    ring = [local_bias]
+    for hop in range(3):
+        ring.append(lax.ppermute(ring[-1], "cols", [(dev, (dev + 1) % 4) for dev in range(4)]))
+    bias_part = jnp.roll(
+        jnp.concatenate(ring[::-1], axis=1), (lax.axis_index("cols") + 1) * ring[0].shape[1], axis=1
+    )
     full_bias, full_mask = (
         lax.all_gather(bias_part, "rows", axis=2, tiled=True),
         lax.all_gather(token_mask.astype(jnp.float32), "rows", axis=0, tiled=True),

time: 86.4 us -> 83.4 us (0.965)
  blocking collectives: 45.7 us -> 31.8 us
  starting transfers between devices: 4.24 us -> 9.76 us
  waiting for transfers between devices: 0.01 us -> 4.88 us
    all_gather x1 -> x0, blocking collectives: 15.8 us -> none  [whole_row_layer(): bias_part = lax.all_gather(local_bias, 'cols', axis=1, tiled=True)]
    ppermute x0 -> x3, starting transfers between devices: none -> 6.28 us  [whole_row_layer(): lax.ppermute(ring[-1], 'cols', [(dev, (dev + 1) % 4) for dev in range(4)])]
    ppermute x0 -> x3, waiting for transfers between devices: none -> 4.88 us  [whole_row_layer(): lax.ppermute(ring[-1], 'cols', [(dev, (dev + 1) % 4) for dev in range(4)])]
    unnamed x1, blocking collectives: 5.63 us -> 7.9 us
  transfers between devices with their start and end apart: 1 -> 4, of which waited for: 0 -> 1; matrix products, arithmetic and copies ran while one was open for 4% -> 1% of each run, Pallas kernels for 0% -> 0%
where the time goes in v1:
time: 83.4 us; the launch traced here: 82.9 us
  blocking collectives  31.8 us (38%)
  matrix products  21.1 us (25%)
  local copies, waits for them, and re-layouts  10.1 us (12%)
  starting transfers between devices  9.76 us (12%)
  waiting for transfers between devices  4.88 us (6%)
  other arithmetic  4.22 us (5%)
  between operations  0.95 us (1%)
    all_to_all x1, blocking collectives, whole_row_layer(): lax.all_to_all(gated_all, 'rows', split_axis=1, concat_axis=0, tiled=True)  15.2 us
    sub x2, matrix products, one_block(): expo = jnp.exp(scores - highest)  8.87 us
    all_gather x1, blocking collectives, whole_row_layer(): lax.all_gather(bias_part, 'rows', axis=2, tiled=True)  8.7 us
    unnamed x1, blocking collectives  7.9 us
    ppermute x3, starting transfers between devices, whole_row_layer(): lax.ppermute(ring[-1], 'cols', [(dev, (dev + 1) % 4) for dev in range(4)])  6.28 us
    dot_general x2, matrix products, one_block(): jnp.einsum('hijk,ikhd->ijhd', weights, values, preferred_element_type=jnp...  5.81 us
    ppermute x3, waiting for transfers between devices, whole_row_layer(): lax.ppermute(ring[-1], 'cols', [(dev, (dev + 1) % 4) for dev in range(4)])  4.88 us
    all_to_all x1, starting transfers between devices, whole_row_layer(): lax.all_to_all(normed, 'rows', split_axis=0, concat_axis=1, tiled=True)  3.48 us
  transfers between devices with their start and end apart: 4, of which 1 were waited for; matrix products, arithmetic and copies ran while one was open for 1% of the time, Pallas kernels for 0%

profile of v1, /device:TPU:0, one launch (start us, length us, event | category | flops | bytes accessed | tf_op | source)
XLA Modules:
  0.0 82.9 jit_solution(17491822389917839355)
XLA Ops:
  0.0 1.7 %reduce_sum.31 = f32[48,48]{1,0:T(8,128)S(1)} reduce(f32[48,48,128]{2,1,0:T(8,128)} %param.13, f32[]{:T(128)} %constant.79.clone.1), dimensions={2}, to_apply=%region_0.0 | reduce | flops 292608 | bytes 1188868 | tf_op jit(solution)/shard_map/reduce_sum | solution.py:11
  1.8 0.7 multiply_reduce_fusion
  2.5 0.0 copy-start.7
  2.5 1.5 %add_convert_fusion = bf16[48,48,128]{2,1,0:T(8,128)(2,1)} fusion(f32[48,48,128]{2,1,0:T(8,128)S(1)} %copy-done.1, f32[128]{0:T(128)S(1)} %copy-done.8, f32[128]{0:T(128)S(1)} %copy-done.9, f32[48,48]{1,0:T(8,128)S(1)} %add_rsqrt_fusion, f32[48,48]{1,0:T(8,128)S(1)} %broadcast_multiply_fusion), kind=kLoop, calls=%fused_computation.31 | loop fusion | flops 1474560 | bytes 1788928 | tf_op jit(solution)/shard_map/convert_element_type | solution.py:14
  4.0 2.9 %convolution_bitcast_fusion = f32[4,48,48]{2,0,1:T(4,128)S(1)} fusion(bf16[48,48,128]{2,1,0:T(8,128)(2,1)} %add_convert_fusion, f32[128,4]{0,1:T(4,128)S(1)} %copy-done.7), kind=kOutput, calls=%fused_computation.33 | convolution fusion | flops 14155776 | bytes 628736 | tf_op jit(solution)/shard_map/dot_general | solution.py:27
  6.9 3.1 %collective-permute-start = (f32[4,48,48]{2,0,1:T(4,128)S(1)}, f32[4,48,48]{2,0,1:T(4,128)S(1)}, u32[]{:S(2)}, u32[]{:S(2)}) collective-permute-start(f32[4,48,48]{2,0,1:T(4,128)S(1)} %convolution_bitcast_fusion), channel_id=1, source_target_pairs={{0,1},{1,2},{2,3},{3,0},{4,5},{5,6},{6,7},{7,4},{8,9},{9,10},{10,1... | collective-permute-start | bytes 110600 | tf_op jit(solution)/shard_map/ppermute | solution.py:34
  10.0 3.5 %all-to-all-start = ((bf16[48,48,128]{2,1,0:T(8,128)(2,1)}), bf16[48,48,128]{2,1,0:T(8,128)(2,1)S(1)}, u32[]{:S(2)}, u32[]{:S(2)}) async-start(bf16[48,48,128]{2,1,0:T(8,128)(2,1)} %add_convert_fusion), calls=%async_computation | async-start | bytes 1179648 | tf_op jit(solution)/shard_map/all_to_all | solution.py:30
  13.5 0.7 dynamic-slice
  14.8 1.6 %collective-permute-start.1 = (f32[4,48,48]{2,0,1:T(4,128)S(1)}, f32[4,48,48]{2,0,1:T(4,128)S(1)}, u32[]{:S(2)}, u32[]{:S(2)}) collective-permute-start(f32[4,48,48]{2,0,1:T(4,128)S(1)} %collective-permute-done), channel_id=1, source_target_pairs={{0,1},{1,2},{2,3},{3,0},{4,5},{5,6},{6,7},{7,4},{8,9},{9,10},{10,1... | collective-permute-start | bytes 110600 | tf_op jit(solution)/shard_map/ppermute | solution.py:34
  16.5 0.1 convert_dynamic-update-slice_fusion
  16.6 7.9 %all-reduce = f32[192]{0:T(256)S(1)} all-reduce(f32[192]{0:T(256)S(1)} %convert_dynamic-update-slice_fusion), channel_id=1, replica_groups=mesh['groups'=2,'rows'=4,'cols'=4] {'rows'}, use_global_device_ids=true, to_apply=%add | all-reduce | flops 192 | bytes 1536
  24.5 1.6 %collective-permute-start.2 = (f32[4,48,48]{2,0,1:T(4,128)S(1)}, f32[4,48,48]{2,0,1:T(4,128)S(1)}, u32[]{:S(2)}, u32[]{:S(2)}) collective-permute-start(f32[4,48,48]{2,0,1:T(4,128)S(1)} %collective-permute-done.1), channel_id=1, source_target_pairs={{0,1},{1,2},{2,3},{3,0},{4,5},{5,6},{6,7},{7,4},{8,9},{9,10},{10,1... | collective-permute-start | bytes 110600 | tf_op jit(solution)/shard_map/ppermute | solution.py:34
  26.0 4.9 %collective-permute-done.2 = f32[4,48,48]{2,0,1:T(4,128)S(1)} collective-permute-done((f32[4,48,48]{2,0,1:T(4,128)S(1)}, f32[4,48,48]{2,0,1:T(4,128)S(1)}, u32[]{:S(2)}, u32[]{:S(2)}) %collective-permute-start.2) | collective-permute-done | bytes 36896 | tf_op jit(solution)/shard_map/ppermute | solution.py:34
  31.1 0.2 copy.58
  31.3 8.7 %all_gather.7 = f32[4,192,192]{1,0,2:T(4,128)S(1)} all-gather(f32[4,192,48]{1,0,2:T(4,128)S(1)} %copy.58), channel_id=1, replica_groups=mesh['groups'=2,'rows'=4,'cols'=4] {'rows'}, dimensions={2}, use_global_device_ids=true | all-gather | bytes 737280 | tf_op jit(solution)/shard_map/all_gather | solution.py:39
  40.0 0.1 copy.55
  40.1 0.4 convolution_convert_fusion
  40.6 0.3 fusion.39
  40.9 0.3 copy.57
  41.2 1.0 %copy.62 = bf16[12,192,4,32]{1,3,0,2:T(8,128)(2,1)} copy(bf16[12,192,4,32]{1,3,2,0:T(8,128)(2,1)S(1)} %bitcast.59) | data formatting | bytes 1179648 | tf_op jit(solution)/shard_map/while | solution.py:72
  42.1 1.2 %copy.59 = bf16[12,192,128]{1,2,0:T(8,128)(2,1)} copy(bf16[12,192,128]{2,1,0:T(8,128)(2,1)S(1)} %get-tuple-element.196) | data formatting | bytes 1179648 | tf_op jit(solution)/shard_map/slice | solution.py:48
  43.3 0.3 fusion.28
  43.6 1.2 %copy.56 = bf16[12,192,128]{1,2,0:T(8,128)(2,1)} copy(bf16[12,192,128]{2,1,0:T(8,128)(2,1)S(1)} %fusion.28) | data formatting | bytes 1179648 | tf_op jit(solution)/shard_map/convert_element_type | solution.py:44
  44.8 1.5 %fusion.27 = f32[12,192,128]{2,1,0:T(8,128)} fusion(bf16[12,192,128]{2,1,0:T(8,128)(2,1)S(1)} %bitcast.58, f32[128]{0:T(128)S(1)} %copy-done.13, bf16[128,128]{1,0:T(8,128)(2,1)S(1)} %copy-done.11), kind=kOutput, calls=%fused_computation.29 | convolution fusion | flops 76677120 | bytes 1802752 | tf_op jit(solution)/shard_map/dot_general | solution.py:49
  46.3 1.0 %broadcast_in_dim.45.clone = bf16[12,192,128]{2,0,1:T(8,128)(2,1)} broadcast(bf16[]{:T(256)} %constant.78.clone.1), dimensions={} | broadcast | bytes 589826 | tf_op jit(solution)/shard_map/broadcast_in_dim | solution.py:76
  47.3 18.9 %while.13 = (s32[]{:T(128)}, bf16[12,192,128]{2,0,1:T(8,128)(2,1)}, f32[12,192,128]{2,1,0:T(8,128)}, pred[192]{0:T(512)(128)(4,1)S(1)}, bf16[12,192,4,32]{1,3,2,...) while((s32[]{:T(128)}, bf16[12,192,128]{2,0,1:T(8,128)(2,1)}, ...), condition=%wide.region_5.6_spmd, body=%wide.region_2.5_spmd.sunk | while | flops 118112448 | bytes 19440052 | solution.py:72
  47.3 0.3 constant_dynamic-slice_fusion.14
  47.6 0.2 copy.100
  47.8 4.4 %fusion.59 = (f32[4,12,96]{2,1,0:T(8,128)S(1)}, bf16[4,12,96,192]{3,2,1,0:T(8,128)(2,1)}) fusion(f32[4,96,192]{2,1,0:T(8,128)S(1)} %copy.100, pred[192]{0:T(512)(128)(4,1)S(1)} %get-tuple-element.278, bf16[12,192,4,32]{1,3,0,2:T(8,128)(2,1)S(1)} %get-tuple-element.280, bf16[12,192,4,32]{1,3,2,0:T(8,128)(2,1)} %get-tuple-element.279, s32[]{:T(128)S(6)} %select_n.46), kind=kOutput, calls=%fused_computation.52.clone.1 | convolution fusion | flops 61046976 | bytes 3066052 | tf_op jit(solution)/shard_map/while/body/eval_jaxpr/sub | solution.py:64
  52.3 2.9 %fusion.60 = f32[12,96,4,32]{1,3,2,0:T(8,128)S(1)} fusion(bf16[12,192,4,32]{1,3,2,0:T(8,128)(2,1)} %get-tuple-element.282, bf16[4,12,96,192]{3,2,1,0:T(8,128)(2,1)} %get-tuple-element.249, f32[12,96,4]{1,2,0:T(4,128)S(1)} %copy.101), kind=kOutput, calls=%fused_computation.10.clone.1 | convolution fusion | flops 56770560 | bytes 2967552 | tf_op jit(solution)/shard_map/while/body/eval_jaxpr/hijk,ikhd->ijhd/dot_general | solution.py:67
  55.2 0.1 constant_dynamic-slice_fusion.13
  55.2 0.3 copy.99
  55.5 0.1 fusion.61
  55.6 0.3 copy.102
  56.0 0.8 constant_dynamic-update-slice_fusion.10
  56.8 0.3 constant_dynamic-slice_fusion.14
  57.1 0.2 copy.100
  57.3 4.4 %fusion.59 = (f32[4,12,96]{2,1,0:T(8,128)S(1)}, bf16[4,12,96,192]{3,2,1,0:T(8,128)(2,1)}) fusion(f32[4,96,192]{2,1,0:T(8,128)S(1)} %copy.100, pred[192]{0:T(512)(128)(4,1)S(1)} %get-tuple-element.278, bf16[12,192,4,32]{1,3,0,2:T(8,128)(2,1)S(1)} %get-tuple-element.280, bf16[12,192,4,32]{1,3,2,0:T(8,128)(2,1)} %get-tuple-element.279, s32[]{:T(128)S(6)} %select_n.46), kind=kOutput, calls=%fused_computation.52.clone.1 | convolution fusion | flops 61046976 | bytes 3066052 | tf_op jit(solution)/shard_map/while/body/eval_jaxpr/sub | solution.py:64
  61.7 0.0 copy-start.2
  61.7 2.9 %fusion.60 = f32[12,96,4,32]{1,3,2,0:T(8,128)S(1)} fusion(bf16[12,192,4,32]{1,3,2,0:T(8,128)(2,1)} %get-tuple-element.282, bf16[4,12,96,192]{3,2,1,0:T(8,128)(2,1)} %get-tuple-element.249, f32[12,96,4]{1,2,0:T(4,128)S(1)} %copy.101), kind=kOutput, calls=%fused_computation.10.clone.1 | convolution fusion | flops 56770560 | bytes 2967552 | tf_op jit(solution)/shard_map/while/body/eval_jaxpr/hijk,ikhd->ijhd/dot_general | solution.py:67
  64.6 0.1 constant_dynamic-slice_fusion.13
  64.7 0.3 copy.99
  65.0 0.1 fusion.61
  65.1 0.3 copy.102
  65.4 0.8 constant_dynamic-update-slice_fusion.10
  66.2 15.2 %all_to_all.36 = bf16[12,192,128]{2,0,1:T(8,128)(2,1)S(1)} all-to-all(bf16[12,192,128]{2,0,1:T(8,128)(2,1)} %get-tuple-element.290), channel_id=1, replica_groups=mesh['groups'=2,'rows'=4,'cols'=4] {'rows'}, dimensions={1} | all-to-all | bytes 1179648 | tf_op jit(solution)/shard_map/all_to_all | solution.py:78
  81.4 0.2 copy.66
  81.6 1.3 %convolution_add_fusion = f32[48,48,128]{2,1,0:T(8,128)} fusion(bf16[48,48,128]{2,1,0:T(8,128)(2,1)S(1)} %bitcast.62, f32[128]{0:T(128)S(1)} %copy-done.10, bf16[128,128]{1,0:T(8,128)(2,1)S(1)} %copy-done.5), kind=kOutput, calls=%fused_computation.23 | convolution fusion | flops 75792384 | bytes 1802752 | tf_op jit(solution)/shard_map/dot_general | solution.py:79
  (50 shorter events, 0.3 us)
Async XLA Ops:
  0.0 40.1 %copy-start = (bf16[128,256]{1,0:T(8,128)(2,1)S(1)}, bf16[128,256]{1,0:T(8,128)(2,1)}, u32[]{:S(2)}) copy-start(bf16[128,256]{1,0:T(8,128)(2,1)} %param.18) | copy-start | bytes 196612
  0.0 1.8 %copy-start.1 = (f32[48,48,128]{2,1,0:T(8,128)S(1)}, f32[48,48,128]{2,1,0:T(8,128)}, u32[]{:S(2)}) copy-start(f32[48,48,128]{2,1,0:T(8,128)} %param.13) | copy-start | bytes 3538948
  0.0 2.5 %copy-start.9 = (f32[128]{0:T(128)S(1)}, f32[128]{0:T(128)}, u32[]{:S(2)}) copy-start(f32[128]{0:T(128)} %param.15) | copy-start | bytes 1540
  0.0 2.5 %copy-start.8 = (f32[128]{0:T(128)S(1)}, f32[128]{0:T(128)}, u32[]{:S(2)}) copy-start(f32[128]{0:T(128)} %param.16) | copy-start | bytes 1540
  2.5 1.6 %copy-start.7 = (f32[128,4]{0,1:T(4,128)S(1)}, f32[128,4]{0,1:T(4,128)}, u32[]{:S(2)}) copy-start(f32[128,4]{0,1:T(4,128)} %param.21) | copy-start | bytes 6148
  4.0 9.4 %copy-start.14 = (u32[32]{0:T(128)S(1)}, u32[32]{0:T(128)}, u32[]{:S(2)}) copy-start(u32[32]{0:T(128)} %constant.92) | copy-start | bytes 388
  4.0 12.4 %copy-start.12 = (s32[48]{0:T(128)S(1)}, s32[48]{0:T(128)}, u32[]{:S(2)}) copy-start(s32[48]{0:T(128)} %param.14) | copy-start | bytes 580
  6.9 7.9 %collective-permute-start = (f32[4,48,48]{2,0,1:T(4,128)S(1)}, f32[4,48,48]{2,0,1:T(4,128)S(1)}, u32[]{:S(2)}, u32[]{:S(2)}) collective-permute-start(f32[4,48,48]{2,0,1:T(4,128)S(1)} %convolution_bitcast_fusion), channel_id=1, source_target_pairs={{0,1},{1,2},{2,3},{3,0},{4,5},{5,6},{6,7},{7,4},{8,9},{9,10},{10,1... | collective-permute-start | bytes 110600 | tf_op jit(solution)/shard_map/ppermute | solution.py:34
  10.0 30.1 %all-to-all-start = ((bf16[48,48,128]{2,1,0:T(8,128)(2,1)}), bf16[48,48,128]{2,1,0:T(8,128)(2,1)S(1)}, u32[]{:S(2)}, u32[]{:S(2)}) async-start(bf16[48,48,128]{2,1,0:T(8,128)(2,1)} %add_convert_fusion), calls=%async_computation | async-start | bytes 1179648 | tf_op jit(solution)/shard_map/all_to_all | solution.py:30
  14.8 9.6 %collective-permute-start.1 = (f32[4,48,48]{2,0,1:T(4,128)S(1)}, f32[4,48,48]{2,0,1:T(4,128)S(1)}, u32[]{:S(2)}, u32[]{:S(2)}) collective-permute-start(f32[4,48,48]{2,0,1:T(4,128)S(1)} %collective-permute-done), channel_id=1, source_target_pairs={{0,1},{1,2},{2,3},{3,0},{4,5},{5,6},{6,7},{7,4},{8,9},{9,10},{10,1... | collective-permute-start | bytes 110600 | tf_op jit(solution)/shard_map/ppermute | solution.py:34
  24.5 6.5 %collective-permute-start.2 = (f32[4,48,48]{2,0,1:T(4,128)S(1)}, f32[4,48,48]{2,0,1:T(4,128)S(1)}, u32[]{:S(2)}, u32[]{:S(2)}) collective-permute-start(f32[4,48,48]{2,0,1:T(4,128)S(1)} %collective-permute-done.1), channel_id=1, source_target_pairs={{0,1},{1,2},{2,3},{3,0},{4,5},{5,6},{6,7},{7,4},{8,9},{9,10},{10,1... | collective-permute-start | bytes 110600 | tf_op jit(solution)/shard_map/ppermute | solution.py:34
  41.2 2.2 %copy-start.6 = (bf16[128,128]{1,0:T(8,128)(2,1)S(1)}, bf16[128,128]{1,0:T(8,128)(2,1)}, u32[]{:S(2)}) copy-start(bf16[128,128]{1,0:T(8,128)(2,1)} %param.17) | copy-start | bytes 98308
  43.3 1.5 %copy-start.11 = (bf16[128,128]{1,0:T(8,128)(2,1)S(1)}, bf16[128,128]{1,0:T(8,128)(2,1)}, u32[]{:S(2)}) copy-start(bf16[128,128]{1,0:T(8,128)(2,1)} %param.19) | copy-start | bytes 98308
  43.3 1.5 %copy-start.13 = (f32[128]{0:T(128)S(1)}, f32[128]{0:T(128)}, u32[]{:S(2)}) copy-start(f32[128]{0:T(128)} %param.20) | copy-start | bytes 1540
  44.8 2.5 %copy-start.3 = (bf16[12,192,4,32]{1,3,0,2:T(8,128)(2,1)S(1)}, bf16[12,192,4,32]{1,3,0,2:T(8,128)(2,1)}, u32[]{:S(2)}) copy-start(bf16[12,192,4,32]{1,3,0,2:T(8,128)(2,1)} %copy.62) | copy-start | bytes 1769476
  52.3 2.9 %copy-start.2 = (f32[12,192,128]{2,1,0:T(8,128)S(1)}, f32[12,192,128]{2,1,0:T(8,128)}, u32[]{:S(2)}) copy-start(f32[12,192,128]{2,1,0:T(8,128)} %get-tuple-element.277) | copy-start | bytes 3538948 | tf_op jit(solution)/shard_map/while
  55.6 1.2 %copy-start.4 = (bf16[12,192,4,32]{1,3,0,2:T(8,128)(2,1)S(1)}, bf16[12,192,4,32]{1,3,0,2:T(8,128)(2,1)}, u32[]{:S(2)}) copy-start(bf16[12,192,4,32]{1,3,0,2:T(8,128)(2,1)} %get-tuple-element.301) | copy-start | bytes 1769476 | tf_op jit(solution)/shard_map/while
  61.7 2.9 %copy-start.2 = (f32[12,192,128]{2,1,0:T(8,128)S(1)}, f32[12,192,128]{2,1,0:T(8,128)}, u32[]{:S(2)}) copy-start(f32[12,192,128]{2,1,0:T(8,128)} %get-tuple-element.277) | copy-start | bytes 3538948 | tf_op jit(solution)/shard_map/while
  65.1 1.2 %copy-start.4 = (bf16[12,192,4,32]{1,3,0,2:T(8,128)(2,1)S(1)}, bf16[12,192,4,32]{1,3,0,2:T(8,128)(2,1)}, u32[]{:S(2)}) copy-start(bf16[12,192,4,32]{1,3,0,2:T(8,128)(2,1)} %get-tuple-element.301) | copy-start | bytes 1769476 | tf_op jit(solution)/shard_map/while
  66.2 15.4 %copy-start.5 = (bf16[128,128]{1,0:T(8,128)(2,1)S(1)}, bf16[128,128]{1,0:T(8,128)(2,1)}, u32[]{:S(2)}) copy-start(bf16[128,128]{1,0:T(8,128)(2,1)} %param.22) | copy-start | bytes 98308
  66.2 15.4 %copy-start.10 = (f32[128]{0:T(128)S(1)}, f32[128]{0:T(128)}, u32[]{:S(2)}) copy-start(f32[128]{0:T(128)} %param.23) | copy-start | bytes 1540
